TPU v7x, 32 devices: a whole 2x2x4 slice. The times are simulated.
32 devices in a mesh: brick: 8 (over y, x, core), help: 4 (over z).
Axes of the slice: x: 2, y: 2, z: 4, core: 2. Of those that a mesh axis runs over, the one named last changes fastest.
Arguments:
- positions: float32 [3, 2048], P(None, ('brick', 'help')), may hold values from 0 to 1
- velocities: float32 [3, 2048], P(None, ('brick', 'help')), may hold values from -5 to 5
- forces_in: float32 [3, 2048], P(None, ('brick', 'help')), may hold values from -5 to 5
- neighbors: int32 [2048, 128], P(('brick', 'help')), may hold values from -1 to 767, as said below
- w_embed1: float32 [32], replicated, may hold values from -4 to 4
- b_embed1: float32 [32], replicated, may hold values from -3 to 3
- w_embed2: bfloat16 [32, 64], replicated, may hold values from -1 to 1
- b_embed2: float32 [64], replicated, may hold values from -3 to 3
- w_embed3: bfloat16 [64, 128], replicated, may hold values from -0.75 to 0.75
- b_embed3: float32 [128], replicated, may hold values from -3 to 3
- w_fit1: bfloat16 [2048, 240], replicated, may hold values from -0.125 to 0.125
- b_fit1: float32 [240], replicated, may hold values from -3 to 3
- w_fit2: bfloat16 [240, 240], replicated, may hold values from -0.375 to 0.375
- b_fit2: float32 [240], replicated, may hold values from -3 to 3
- w_out: float32 [240], replicated, may hold values from -0.375 to 0.375
Outputs:
- positions_out: float32 [3, 2048], P(None, ('brick', 'help'))
- velocities_out: float32 [3, 2048], P(None, ('brick', 'help'))
- energy: float32 [2048], P(('brick', 'help'))
- forces_out: float32 [3, 2048], P(None, ('brick', 'help'))
Inputs may be any that keep to these rules, and one draw needn't show every extreme that they name: `neighbors`: row i holds atom i's neighbours as table entries: 0 to 255 the atoms of the brick before its own (cyclically), 256 to 511 its own brick, 512 to 767 the brick after; -1 pads. Live entries come first, an entry may repeat, an atom never lists itself. In the first half of the bricks an atom has 96 to 128 live entries, in the other bricks 128 / 4 to 64.
All inputs are finite; a program needn't handle non-finite values.
Results may differ from a plain program's by a relative error of at most 0.011.
Values sent between devices are 32-bit elements; how exact they have to be, the bound alone decides.
No kernel may reach another device: no remote copies, remote signals or barrier semaphores. Data moves between devices by JAX's collectives and lax.ppermute only.
A program may use at most 64 MiB of HBM per device.

v0:
```python
import jax
import jax.numpy as jnp
from jax import lax
from jax.sharding import PartitionSpec as P

NEIGHBOUR_SLOTS = 128
M2 = 16
STEPS = 2
kick_scale = 0.25
time_step = 0.05
highest_precision = lax.Precision.HIGHEST


def extended(value, sides, width):
    for axis, dim in sides:
        size, length = (lax.axis_size(axis), value.shape[dim])
        up = [(i, (i + 1) % size) for i in range(size)]
        down = [(j, i) for i, j in up]
        last = lax.slice_in_dim(value, length - width, length, axis=dim)
        first = lax.slice_in_dim(value, 0, width, axis=dim)
        before = lax.ppermute(last, axis, up)
        after = lax.ppermute(first, axis, down)
        value = jnp.concatenate([before, value, after], axis=dim)
    return value


def pair_terms(displace, live_mask, weights):
    (
        w_embed1,
        b_embed1,
        w_embed2,
        b_embed2,
        w_embed3,
        b_embed3,
        w_fit1,
        b_fit1,
        w_fit2,
        b_fit2,
        w_out,
    ) = weights
    blocks, slot_count = live_mask.shape
    quad_dist = jnp.sum(displace * displace, axis=0) + 0.25
    radius = jnp.sqrt(quad_dist)
    smooth = live_mask / radius
    environment_matrix = jnp.concatenate(
        [smooth[None], live_mask[None] * displace / quad_dist[None]], axis=0
    ).astype(jnp.bfloat16)
    flat_smooth = smooth.reshape(1, -1)
    hidden_first = jnp.tanh(w_embed1[:, None] * flat_smooth + b_embed1[:, None])
    pre_second = (
        jnp.dot(w_embed2.T, hidden_first.astype(jnp.bfloat16), preferred_element_type=jnp.float32)
        + b_embed2[:, None]
    )
    tanh_second = jnp.tanh(pre_second)
    hidden_second = jnp.concatenate([hidden_first, hidden_first], axis=0) + tanh_second
    pre_third = (
        jnp.dot(w_embed3.T, hidden_second.astype(jnp.bfloat16), preferred_element_type=jnp.float32)
        + b_embed3[:, None]
    )
    tanh_third = jnp.tanh(pre_third)
    embedding = (jnp.concatenate([hidden_second, hidden_second], axis=0) + tanh_third).astype(
        jnp.bfloat16
    )
    embedding_width = embedding.shape[0]
    embedding_rows = embedding.reshape(embedding_width, blocks, slot_count)
    descriptor_tensor = (
        jnp.einsum(
            "srj,lrj->rsl", environment_matrix, embedding_rows, preferred_element_type=jnp.float32
        )
        / NEIGHBOUR_SLOTS
    )
    axis_part = descriptor_tensor[:, :, :M2]
    descriptor = jnp.einsum(
        "bce,bck->bek", descriptor_tensor, axis_part, precision=highest_precision
    )
    flat_descr = descriptor.reshape(blocks, -1).astype(jnp.bfloat16)
    fit_hidden = jnp.tanh(jnp.dot(flat_descr, w_fit1, preferred_element_type=jnp.float32) + b_fit1)
    pre_out = (
        jnp.dot(fit_hidden.astype(jnp.bfloat16), w_fit2, preferred_element_type=jnp.float32)
        + b_fit2
    )
    tanh_out = jnp.tanh(pre_out)
    energy = jnp.dot(fit_hidden + tanh_out, w_out, precision=highest_precision)
    grad_out = (w_out[None, :] * (1.0 - tanh_out * tanh_out)).astype(jnp.bfloat16)
    grad_fit = w_out[None, :] + jnp.dot(grad_out, w_fit2.T, preferred_element_type=jnp.float32)
    grad_act = (grad_fit * (1.0 - fit_hidden * fit_hidden)).astype(jnp.bfloat16)
    grad_descr = jnp.dot(grad_act, w_fit1.T, preferred_element_type=jnp.float32).reshape(
        blocks, embedding_width, -1
    )
    grad_tensor = jnp.einsum("bek,bck->bce", grad_descr, axis_part, precision=highest_precision)
    extra_grad = jnp.einsum(
        "bek,bce->bck", grad_descr, descriptor_tensor, precision=highest_precision
    )
    grad_tensor = grad_tensor + jnp.pad(
        extra_grad, ((0, 0), (0, 0), (0, embedding_width - extra_grad.shape[2]))
    )
    descriptor_product_gradient = grad_tensor.astype(jnp.bfloat16)
    environment_gradient = (
        jnp.einsum(
            "ohm,hdo->dhm",
            embedding_rows,
            descriptor_product_gradient,
            preferred_element_type=jnp.float32,
        )
        / NEIGHBOUR_SLOTS
    )
    embedding_gradient = (
        jnp.einsum(
            "zmj,mzr->rmj",
            environment_matrix,
            descriptor_product_gradient,
            preferred_element_type=jnp.float32,
        ).reshape(embedding_width, -1)
        / NEIGHBOUR_SLOTS
    )
    grad_third = (embedding_gradient * (1.0 - tanh_third * tanh_third)).astype(jnp.bfloat16)
    half_width = embedding_width // 2
    grad_hidden2 = (
        embedding_gradient[:half_width]
        + embedding_gradient[half_width:]
        + jnp.dot(w_embed3, grad_third, preferred_element_type=jnp.float32)
    )
    grad_second = (grad_hidden2 * (1.0 - tanh_second * tanh_second)).astype(jnp.bfloat16)
    quarter = half_width // 2
    grad_hidden1 = (
        grad_hidden2[:quarter]
        + grad_hidden2[quarter:]
        + jnp.dot(w_embed2, grad_second, preferred_element_type=jnp.float32)
    )
    grad_smooth = (
        jnp.dot(
            w_embed1,
            grad_hidden1 * (1.0 - hidden_first * hidden_first),
            precision=highest_precision,
        ).reshape(blocks, slot_count)
        + environment_gradient[0]
    )
    radial = jnp.sum(environment_gradient[1:] * displace, axis=0)
    factor = -grad_smooth / (radius * quad_dist) - 2.0 * radial / (quad_dist * quad_dist)
    pair_grad = live_mask[None] * (
        displace * factor[None] + environment_gradient[1:] / quad_dist[None]
    )
    return (energy, pair_grad)


def ghost_table(coords):
    stacked = coords[:, None, :]
    brick_pos = lax.all_gather(stacked, "help", axis=2, tiled=True)
    gathered = extended(brick_pos, (("brick", 1),), 1)
    return gathered.reshape(3, -1)


def return_forces(gathered):
    reduced = lax.psum_scatter(gathered, "help", scatter_dimension=2, tiled=True)
    padded = extended(reduced, (("brick", 1),), 1)
    returned = padded[:, 0] + padded[:, 2] + padded[:, 4]
    return returned


def evaluate(coords, neighbors, weights):
    ghost = ghost_table(coords)
    brick_len = ghost.shape[1] // 3
    atom_count = coords.shape[1]
    safe_index = jnp.maximum(neighbors, 0)
    live_mask = (neighbors >= 0).astype(jnp.float32)
    shift_x = (safe_index // brick_len - 1).astype(jnp.float32)
    block_size = 32
    block_count = atom_count // block_size

    def one_block(pieces):
        own_pos, table_index, offset, mask_rows = pieces
        neighbour_pos = jnp.take(ghost, table_index, axis=1)
        displace = neighbour_pos - own_pos[:, :, None]
        displace = (
            jnp.concatenate([displace[:1] + offset[None], displace[1:]], axis=0) * mask_rows[None]
        )
        return pair_terms(displace, mask_rows, weights)

    own_blocks = coords.reshape(3, block_count, block_size).transpose(1, 0, 2)
    energy, pair_grads = lax.map(
        one_block,
        (
            own_blocks,
            safe_index.reshape(block_count, block_size, -1),
            shift_x.reshape(block_count, block_size, -1),
            live_mask.reshape(block_count, block_size, -1),
        ),
    )
    pair_grads = pair_grads.transpose(1, 0, 2, 3).reshape(3, atom_count, -1)
    energy_rows = energy.reshape(-1)
    gathered = jnp.zeros((3, 3 * brick_len), jnp.float32).at[:, safe_index].add(pair_grads)
    returned = return_forces(gathered.reshape(3, 3, brick_len))
    return (energy_rows, jnp.sum(pair_grads, axis=2) - returned)


def local(
    positions,
    velocities,
    forces_in,
    neighbors,
    w_embed1,
    b_embed1,
    w_embed2,
    b_embed2,
    w_embed3,
    b_embed3,
    w_fit1,
    b_fit1,
    w_fit2,
    b_fit2,
    w_out,
):
    weights = (
        w_embed1,
        b_embed1,
        w_embed2,
        b_embed2,
        w_embed3,
        b_embed3,
        w_fit1,
        b_fit1,
        w_fit2,
        b_fit2,
        w_out,
    )
    coords = positions
    speed = velocities
    force_now = forces_in
    energy = jnp.zeros((positions.shape[1],), jnp.float32)
    for md_step in range(STEPS):
        speed = speed + kick_scale * force_now
        coords = coords + time_step * speed
        energy, force_now = evaluate(coords, neighbors, weights)
        speed = speed + kick_scale * force_now
    return (coords, speed, energy, force_now)


def solution(mesh):
    return jax.shard_map(
        local,
        mesh=mesh,
        in_specs=(
            P(None, ("brick", "help")),
            P(None, ("brick", "help")),
            P(None, ("brick", "help")),
            P(("brick", "help"), None),
            P(),
            P(),
            P(),
            P(),
            P(),
            P(),
            P(),
            P(),
            P(),
            P(),
            P(),
        ),
        out_specs=(
            P(None, ("brick", "help")),
            P(None, ("brick", "help")),
            P(("brick", "help")),
            P(None, ("brick", "help")),
        ),
        check_vma=False,
    )
```

profile of v0, /device:TPU:0, one launch (start us, length us, event | category | flops | bytes accessed | tf_op | source)
XLA Modules:
  0.0 359.1 jit_solution(11644134132301394717)
XLA Ops:
  7.9 13.6 %all-gather.2 = f32[4,64,3]{1,2,0:T(4,128)S(1)} all-gather(f32[1,64,3]{1,2,0:T(4,128)S(1)} %bitcast.479), channel_id=2, replica_groups=mesh['brick'=8,'help'=4] {'help'}, dimensions={0}, use_global_device_ids=true | all-gather | bytes 3840 | tf_op jit(solution)/shard_map/all_gather | solution.py:148
  26.5 71.5 %while.26 = (s32[]{:T(128)}, f32[2,3,32,128]{3,1,2,0:T(4,128)}, f32[2,32,128]{2,0,1:T(2,128)S(1)}, s32[2,32,128]{2,1,0:T(8,128)}, f32[3,768]{0,1:T(8,128)S(1)}, ...) while((s32[]{:T(128)}, f32[2,3,32,128]{3,1,2,0:T(4,128)}, ...), condition=%wide.region_3.5_spmd, body=%wide.region_0.4_spmd.sunk | while | flops 271267840 | bytes 53851500 | solution.py:180
  27.4 10.8 %gather_fusion = f32[4096,3]{1,0:T(8,128)S(1)} fusion(f32[3,768]{0,1:T(8,128)S(1)} %get-tuple-element.963, s32[4096]{0:T(1024)S(1)} %bitcast_clamp_fusion.4), kind=kCustom, calls=%fused_computation.clone.clone.1 | custom fusion | bytes 114688 | tf_op jit(solution)/shard_map/while/body/eval_jaxpr/jit(_take)/gather | solution.py:172
  40.7 2.1 maximum_add_fusion.6
  51.0 1.5 fusion.267
  52.5 1.8 copy.234
  63.1 10.8 %gather_fusion = f32[4096,3]{1,0:T(8,128)S(1)} fusion(f32[3,768]{0,1:T(8,128)S(1)} %get-tuple-element.963, s32[4096]{0:T(1024)S(1)} %bitcast_clamp_fusion.4), kind=kCustom, calls=%fused_computation.clone.clone.1 | custom fusion | bytes 114688 | tf_op jit(solution)/shard_map/while/body/eval_jaxpr/jit(_take)/gather | solution.py:172
  76.5 2.1 maximum_add_fusion.6
  84.2 1.4 fusion.265
  86.7 1.5 fusion.267
  88.3 1.8 copy.234
  98.0 3.5 copy.144
  101.6 45.3 %scatter_custom_fusion = f32[3,768]{0,1:T(8,128)S(1)} fusion(s32[8192]{0:T(1024)} %get-tuple-element.670, f32[8192,3]{1,0:T(8,128)} %bitcast.458, f32[]{:T(128)} %constant.160.clone.1), kind=kCustom, calls=%fused_computation.189 | custom fusion | flops 24576 | bytes 9728 | tf_op jit(solution)/shard_map/scatter-add | solution.py:191
  148.1 24.3 %reduce-scatter.7.cloned.1.call-done = f32[64,9]{1,0:T(8,128)} async-done(((f32[256,9]{1,0:T(8,128)}), f32[64,9]{1,0:T(8,128)}) %reduce-scatter.7.cloned.1.call-update) | async-done | bytes 2320
  174.7 2.7 collective-permute-done.2
  178.0 11.9 %all-gather.3 = f32[4,64,3]{1,2,0:T(4,128)S(1)} all-gather(f32[1,64,3]{1,2,0:T(4,128)S(1)} %bitcast.480), channel_id=3, replica_groups=mesh['brick'=8,'help'=4] {'help'}, dimensions={0}, use_global_device_ids=true | all-gather | bytes 3840 | tf_op jit(solution)/shard_map/all_gather | solution.py:148
  191.4 2.8 collective-permute-done.4
  195.8 77.6 %while.27 = (s32[]{:T(128)}, f32[2,32]{1,0:T(2,128)}, f32[2,3,32,128]{3,1,2,0:T(4,128)}, f32[2,32,128]{2,0,1:T(2,128)S(1)}, s32[2,32,128]{2,1,0:T(8,128)}, /*ind...) while((s32[]{:T(128)}, f32[2,32]{1,0:T(2,128)}, ...), condition=%wide.region_10.12_spmd, body=%wide.region_7.11_spmd.sunk | while | flops 271367680 | bytes 45020100 | solution.py:180
  196.6 11.8 %gather_fusion.1 = f32[4096,3]{1,0:T(8,128)S(1)} fusion(f32[3,768]{0,1:T(8,128)} %get-tuple-element.1025, s32[4096]{0:T(1024)S(1)} %bitcast_clamp_fusion.5), kind=kCustom, calls=%fused_computation.1.clone.clone.1 | custom fusion | bytes 114688 | tf_op jit(solution)/shard_map/while/body/eval_jaxpr/jit(_take)/gather | solution.py:172
  211.0 2.1 maximum_add_fusion.7
  222.4 2.4 fusion.307
  224.7 1.7 copy.242
  227.3 1.6 fusion.310
  235.4 11.8 %gather_fusion.1 = f32[4096,3]{1,0:T(8,128)S(1)} fusion(f32[3,768]{0,1:T(8,128)} %get-tuple-element.1025, s32[4096]{0:T(1024)S(1)} %bitcast_clamp_fusion.5), kind=kCustom, calls=%fused_computation.1.clone.clone.1 | custom fusion | bytes 114688 | tf_op jit(solution)/shard_map/while/body/eval_jaxpr/jit(_take)/gather | solution.py:172
  249.7 2.1 maximum_add_fusion.7
  261.1 2.4 fusion.307
  263.5 1.7 copy.242
  266.1 1.6 fusion.310
  273.4 3.5 copy.152
  276.9 45.2 %scatter_custom_fusion.1 = f32[3,768]{0,1:T(8,128)S(1)} fusion(s32[8192]{0:T(1024)} %get-tuple-element.670, f32[8192,3]{1,0:T(8,128)} %bitcast.457, f32[]{:T(128)} %constant.160.clone.1), kind=kCustom, calls=%fused_computation.187 | custom fusion | flops 24576 | bytes 9728 | tf_op jit(solution)/shard_map/scatter-add | solution.py:191
  323.3 23.3 %reduce-scatter.9.cloned.1.call-done = f32[64,9]{1,0:T(8,128)} async-done(((f32[256,9]{1,0:T(8,128)}), f32[64,9]{1,0:T(8,128)}) %reduce-scatter.9.cloned.1.call-update) | async-done | bytes 2320
  349.8 1.8 collective-permute-done.6
  (417 shorter events, 92.3 us)
Async XLA Ops:
  7.2 165.2 %reduce-scatter.7.cloned.1.call-start = ((), (), s32[]{:S(2)}) async-start(), calls=%async_computation.2 | async-start | bytes 163840
  7.9 18.6 %copy-start.58 = (f32[3,64]{1,0:T(4,128)}, f32[3,64]{1,0:T(4,128)S(1)}, u32[]{:S(2)}) copy-start(f32[3,64]{1,0:T(4,128)S(1)} %multiply_add_fusion.2) | copy-start | bytes 2308
  21.6 2.8 collective-permute-start.1
  21.7 4.0 %collective-permute-start = (f32[3,1,256]{2,0,1:T(4,128)S(1)}, f32[3,1,256]{2,0,1:T(4,128)S(1)}, u32[]{:S(2)}, u32[]{:S(2)}) collective-permute-start(f32[3,1,256]{2,0,1:T(4,128)S(1)} %bitcast.482), channel_id=1, source_target_pairs={{0,4},{4,8},{8,12},{12,16},{16,20},{20,24},{24,28},{28,0},{1,5},{5... | collective-permute-start | bytes 9224 | tf_op jit(solution)/shard_map/ppermute | solution.py:21
  26.5 16.3 %copy-start.14 = (f32[3,768]{0,1:T(8,128)}, f32[3,768]{0,1:T(8,128)S(1)}, u32[]{:S(2)}) copy-start(f32[3,768]{0,1:T(8,128)S(1)} %get-tuple-element.963) | copy-start | bytes 27652 | tf_op jit(solution)/shard_map/while
  26.5 16.3 %copy-start.36 = (f32[2,32,128]{2,0,1:T(2,128)}, f32[2,32,128]{2,0,1:T(2,128)S(1)}, u32[]{:S(2)}) copy-start(f32[2,32,128]{2,0,1:T(2,128)S(1)} %get-tuple-element.961) | copy-start | bytes 98308 | tf_op jit(solution)/shard_map/while
  26.5 16.3 %copy-start.40 = (f32[2,32,128]{2,0,1:T(2,128)}, f32[2,32,128]{2,0,1:T(2,128)S(1)}, u32[]{:S(2)}) copy-start(f32[2,32,128]{2,0,1:T(2,128)S(1)} %get-tuple-element.965) | copy-start | bytes 98308 | tf_op jit(solution)/shard_map/while
  26.5 16.3 %copy-start.56 = (f32[2,3,32]{2,1,0:T(4,128)}, f32[2,3,32]{2,1,0:T(4,128)S(1)}, u32[]{:S(2)}) copy-start(f32[2,3,32]{2,1,0:T(4,128)S(1)} %get-tuple-element.964) | copy-start | bytes 2308 | tf_op jit(solution)/shard_map/while
  62.3 16.3 %copy-start.14 = (f32[3,768]{0,1:T(8,128)}, f32[3,768]{0,1:T(8,128)S(1)}, u32[]{:S(2)}) copy-start(f32[3,768]{0,1:T(8,128)S(1)} %get-tuple-element.963) | copy-start | bytes 27652 | tf_op jit(solution)/shard_map/while
  62.3 16.3 %copy-start.36 = (f32[2,32,128]{2,0,1:T(2,128)}, f32[2,32,128]{2,0,1:T(2,128)S(1)}, u32[]{:S(2)}) copy-start(f32[2,32,128]{2,0,1:T(2,128)S(1)} %get-tuple-element.961) | copy-start | bytes 98308 | tf_op jit(solution)/shard_map/while
  62.3 16.3 %copy-start.40 = (f32[2,32,128]{2,0,1:T(2,128)}, f32[2,32,128]{2,0,1:T(2,128)S(1)}, u32[]{:S(2)}) copy-start(f32[2,32,128]{2,0,1:T(2,128)S(1)} %get-tuple-element.965) | copy-start | bytes 98308 | tf_op jit(solution)/shard_map/while
  101.5 72.5 %copy-start.49 = (f32[2,3,32,128]{3,1,2,0:T(4,128)S(1)}, f32[2,3,32,128]{3,1,2,0:T(4,128)}, u32[]{:S(2)}) copy-start(f32[2,3,32,128]{3,1,2,0:T(4,128)} %get-tuple-element.460) | copy-start | bytes 294916
  101.5 75.9 %copy-start.59 = (f32[3,64]{1,0:T(4,128)S(1)}, f32[3,64]{1,0:T(4,128)}, u32[]{:S(2)}) copy-start(f32[3,64]{1,0:T(4,128)} %copy-done.58) | copy-start | bytes 2308
  101.5 75.9 %copy-start.62 = (f32[3,64]{1,0:T(4,128)S(1)}, f32[3,64]{1,0:T(4,128)}, u32[]{:S(2)}) copy-start(f32[3,64]{1,0:T(4,128)} %param.22) | copy-start | bytes 2308
  101.5 75.9 %copy-start.63 = (f32[3,64]{1,0:T(4,128)S(1)}, f32[3,64]{1,0:T(4,128)}, u32[]{:S(2)}) copy-start(f32[3,64]{1,0:T(4,128)} %param.23) | copy-start | bytes 2308
  101.5 94.3 %copy-start.1 = (bf16[2048,240]{0,1:T(8,128)(2,1)S(1)}, bf16[2048,240]{0,1:T(8,128)(2,1)}, u32[]{:S(2)}) copy-start(bf16[2048,240]{0,1:T(8,128)(2,1)} %get-tuple-element.1043) | copy-start | bytes 2949124
  101.5 94.3 %copy-start.8 = (bf16[240,240]{1,0:T(8,128)(2,1)S(1)}, bf16[240,240]{1,0:T(8,128)(2,1)}, u32[]{:S(2)}) copy-start(bf16[240,240]{1,0:T(8,128)(2,1)} %get-tuple-element.1044) | copy-start | bytes 345604
  101.5 94.3 %copy-start.35 = (bf16[32,64]{1,0:T(8,128)(2,1)S(1)}, bf16[32,64]{1,0:T(8,128)(2,1)}, u32[]{:S(2)}) copy-start(bf16[32,64]{1,0:T(8,128)(2,1)} %get-tuple-element.1045) | copy-start | bytes 12292
  148.0 198.6 %reduce-scatter.9.cloned.1.call-start = ((), (), s32[]{:S(2)}) async-start(), calls=%async_computation.3 | async-start | bytes 163840
  173.4 1.3 collective-permute-start.3
  173.5 3.9 %collective-permute-start.2 = (f32[3,1,64]{2,0,1:T(4,128)S(1)}, f32[3,1,64]{2,0,1:T(4,128)S(1)}, u32[]{:S(2)}, u32[]{:S(2)}) collective-permute-start(f32[3,1,64]{2,0,1:T(4,128)S(1)} %copy.169), channel_id=1, source_target_pairs={{0,4},{4,8},{8,12},{12,16},{16,20},{20,24},{24,28},{28,0},{1,5},{5... | collective-permute-start | bytes 2312 | tf_op jit(solution)/shard_map/ppermute | solution.py:21
  178.0 17.8 %copy-start.60 = (f32[3,64]{1,0:T(4,128)}, f32[3,64]{1,0:T(4,128)S(1)}, u32[]{:S(2)}) copy-start(f32[3,64]{1,0:T(4,128)S(1)} %get-tuple-element.650) | copy-start | bytes 2308
  190.0 1.3 collective-permute-start.5
  190.0 4.2 %collective-permute-start.4 = (f32[3,1,256]{2,0,1:T(4,128)S(1)}, f32[3,1,256]{2,0,1:T(4,128)S(1)}, u32[]{:S(2)}, u32[]{:S(2)}) collective-permute-start(f32[3,1,256]{2,0,1:T(4,128)S(1)} %bitcast.485), channel_id=1, source_target_pairs={{0,4},{4,8},{8,12},{12,16},{16,20},{20,24},{24,28},{28,0},{1,5},{5... | collective-permute-start | bytes 9224 | tf_op jit(solution)/shard_map/ppermute | solution.py:21
  195.8 17.2 %copy-start.38 = (f32[2,32,128]{2,0,1:T(2,128)}, f32[2,32,128]{2,0,1:T(2,128)S(1)}, u32[]{:S(2)}) copy-start(f32[2,32,128]{2,0,1:T(2,128)S(1)} %get-tuple-element.1023) | copy-start | bytes 98308 | tf_op jit(solution)/shard_map/while
  195.9 17.2 %copy-start.42 = (f32[2,32,128]{2,0,1:T(2,128)}, f32[2,32,128]{2,0,1:T(2,128)S(1)}, u32[]{:S(2)}) copy-start(f32[2,32,128]{2,0,1:T(2,128)S(1)} %get-tuple-element.1027) | copy-start | bytes 98308 | tf_op jit(solution)/shard_map/while
  234.6 17.2 %copy-start.38 = (f32[2,32,128]{2,0,1:T(2,128)}, f32[2,32,128]{2,0,1:T(2,128)S(1)}, u32[]{:S(2)}) copy-start(f32[2,32,128]{2,0,1:T(2,128)S(1)} %get-tuple-element.1023) | copy-start | bytes 98308 | tf_op jit(solution)/shard_map/while
  234.7 17.2 %copy-start.42 = (f32[2,32,128]{2,0,1:T(2,128)}, f32[2,32,128]{2,0,1:T(2,128)S(1)}, u32[]{:S(2)}) copy-start(f32[2,32,128]{2,0,1:T(2,128)S(1)} %get-tuple-element.1027) | copy-start | bytes 98308 | tf_op jit(solution)/shard_map/while
  276.9 71.3 %copy-start.46 = (f32[2,3,32,128]{3,1,2,0:T(4,128)S(1)}, f32[2,3,32,128]{3,1,2,0:T(4,128)}, u32[]{:S(2)}) copy-start(f32[2,3,32,128]{3,1,2,0:T(4,128)} %get-tuple-element.461) | copy-start | bytes 294916
  276.9 74.7 %copy-start.61 = (f32[3,64]{1,0:T(4,128)S(1)}, f32[3,64]{1,0:T(4,128)}, u32[]{:S(2)}) copy-start(f32[3,64]{1,0:T(4,128)} %get-tuple-element.651) | copy-start | bytes 2308
  347.7 2.2 collective-permute-start.7
  347.7 3.9 %collective-permute-start.6 = (f32[3,1,64]{2,0,1:T(4,128)S(1)}, f32[3,1,64]{2,0,1:T(4,128)S(1)}, u32[]{:S(2)}, u32[]{:S(2)}) collective-permute-start(f32[3,1,64]{2,0,1:T(4,128)S(1)} %copy.172), channel_id=1, source_target_pairs={{0,4},{4,8},{8,12},{12,16},{16,20},{20,24},{24,28},{28,0},{1,5},{5... | collective-permute-start | bytes 2312 | tf_op jit(solution)/shard_map/ppermute | solution.py:21
  (95 other events, 311.7 us)
Sparse Core Ops, SparseCore 0:
  148.2 24.1 reduce-scatter.6
  323.5 23.1 reduce-scatter.8
where the time goes:
time: 362 us; the launch traced here: 359 us
  other arithmetic  107 us (30%)
  local copies, waits for them, and re-layouts  87 us (24%)
  matrix products  64.1 us (18%)
  waiting for transfers between devices  57.3 us (16%)
  blocking collectives  25.5 us (7%)
  between operations  14.2 us (4%)
    scatter-add x2, other arithmetic, evaluate(): jnp.zeros((3, 3 * brick_len), jnp.float32).at[:, safe_index].add(pair_grads)  90.5 us
    unnamed x4, waiting for transfers between devices  47.6 us
    gather x8, local copies, waits for them, and re-layouts, one_block(): neighbour_pos = jnp.take(ghost, table_index, axis=1)  47.5 us
    all_gather x2, blocking collectives, ghost_table(): brick_pos = lax.all_gather(stacked, 'help', axis=2, tiled=True)  25.5 us
    while x212, local copies, waits for them, and re-layouts  8.73 us
    ppermute x4, waiting for transfers between devices, extended(): before = lax.ppermute(last, axis, up)  8.48 us
    dot_general x4, matrix products, pair_terms(): jnp.dot(w_embed2.T, hidden_first.astype(jnp.bfloat16), preferred_element_...  8.38 us
    dot_general x4, matrix products, pair_terms(): jnp.dot(grad_act, w_fit1.T, preferred_element_type=jnp.float32)  7.82 us
  transfers between devices with their start and end apart: 10, of which 8 were waited for; matrix products, arithmetic and copies ran while one was open for 1% of the time, Pallas kernels for 0%

commit v1 on v0

--- a/solution.py
+++ b/solution.py
@@ -9,6 +9,28 @@
 kick_scale = 0.25
 time_step = 0.05
 highest_precision = lax.Precision.HIGHEST
+
+
+def joined_along(parts, dim):
+    lengths = list(parts.shape[1:])
+    lengths[dim] *= parts.shape[0]
+    return jnp.moveaxis(parts, 0, dim).reshape(lengths)
+
+
+def collect(x, axis, dim):
+    size = lax.axis_size(axis)
+    pairs = [(i, (i + 1) % size) for i in range(size)]
+    back = [(b, a) for a, b in pairs]
+    lower, upper = ([], [])
+    for step in range(size - 1):
+        if step % 2 == 0:
+            lower.append(lax.ppermute(lower[-1] if lower else x, axis, pairs))
+        else:
+            upper.append(lax.ppermute(upper[-1] if upper else x, axis, back))
+    blocks = jnp.stack([*lower[::-1], x, *upper])
+    shift = lax.axis_index(axis) - len(lower)
+    blocks = blocks[(jnp.arange(size) - shift) % size]
+    return joined_along(blocks, dim)
 
 
 def extended(value, sides, width):
@@ -145,7 +167,7 @@
 
 def ghost_table(coords):
     stacked = coords[:, None, :]
-    brick_pos = lax.all_gather(stacked, "help", axis=2, tiled=True)
+    brick_pos = collect(stacked, "help", 2)
     gathered = extended(brick_pos, (("brick", 1),), 1)
     return gathered.reshape(3, -1)
 

time: 362 us -> 362 us (level)
  blocking collectives: 25.5 us -> 0 us
  waiting for transfers between devices: 57.3 us -> 72.9 us
  starting transfers between devices: 2.13 us -> 11 us
    all_gather x2 -> x0, blocking collectives: 25.5 us -> none  [ghost_table(): brick_pos = lax.all_gather(stacked, 'help', axis=2, tiled=True)]
    ppermute x0 -> x6, waiting for transfers between devices: none -> 16.9 us  [the longest x4 16.9 us: collect(): lower.append(lax.ppermute(lower[-1] if lower else x, axis, pairs))]
    ppermute x0 -> x6, starting transfers between devices: none -> 8.91 us  [the longest x2 8.9 us: collect(): upper.append(lax.ppermute(upper[-1] if upper else x, axis, back))]
  transfers between devices with their start and end apart: 10 -> 16, of which waited for: 8 -> 12; matrix products, arithmetic and copies ran while one was open for 1% -> 1% of each run, Pallas kernels for 0% -> 0%
where the time goes in v1:
time: 362 us; the launch traced here: 359 us
  other arithmetic  107 us (30%)
  local copies, waits for them, and re-layouts  88.1 us (24%)
  waiting for transfers between devices  72.9 us (20%)
  matrix products  64 us (18%)
  between operations  14.3 us (4%)
  starting transfers between devices  11 us (3%)
    scatter-add x2, other arithmetic, evaluate(): jnp.zeros((3, 3 * brick_len), jnp.float32).at[:, safe_index].add(pair_grads)  90.5 us
    gather x8, local copies, waits for them, and re-layouts, one_block(): neighbour_pos = jnp.take(ghost, table_index, axis=1)  47.5 us
    unnamed x4, waiting for transfers between devices  45.8 us
    ppermute x4, waiting for transfers between devices, collect(): lower.append(lax.ppermute(lower[-1] if lower else x, axis, pairs))  16.9 us
    ppermute x4, waiting for transfers between devices, extended(): before = lax.ppermute(last, axis, up)  9.05 us
    ppermute x2, starting transfers between devices, collect(): upper.append(lax.ppermute(upper[-1] if upper else x, axis, back))  8.9 us
    while x212, local copies, waits for them, and re-layouts  8.66 us
    dot_general x4, matrix products, pair_terms(): jnp.dot(w_embed2.T, hidden_first.astype(jnp.bfloat16), preferred_element_...  8.31 us
  transfers between devices with their start and end apart: 16, of which 12 were waited for; matrix products, arithmetic and copies ran while one was open for 1% of the time, Pallas kernels for 0%

profile of v1, /device:TPU:0, one launch (start us, length us, event | category | flops | bytes accessed | tf_op | source)
XLA Modules:
  0.0 359.2 jit_solution(9308263108978907586)
XLA Ops:
  7.9 5.1 %collective-permute-start.2 = (f32[3,1,64]{2,0,1:T(4,128)S(1)}, f32[3,1,64]{2,0,1:T(4,128)S(1)}, u32[]{:S(2)}, u32[]{:S(2)}) collective-permute-start(f32[3,1,64]{2,0,1:T(4,128)S(1)} %bitcast.487), channel_id=1, source_target_pairs={{1,0},{2,1},{3,2},{0,3},{5,4},{6,5},{7,6},{4,7},{9,8},{10,9},{11,1... | collective-permute-start | bytes 2312 | tf_op jit(solution)/shard_map/ppermute | solution.py:29
  13.8 4.6 %collective-permute-done = f32[3,1,64]{2,0,1:T(4,128)S(1)} collective-permute-done((f32[3,1,64]{2,0,1:T(4,128)S(1)}, f32[3,1,64]{2,0,1:T(4,128)S(1)}, u32[]{:S(2)}, u32[]{:S(2)}) %collective-permute-start) | collective-permute-done | bytes 800 | tf_op jit(solution)/shard_map/ppermute | solution.py:27
  18.4 5.4 %collective-permute-done.1 = f32[3,1,64]{2,0,1:T(4,128)S(1)} collective-permute-done((f32[3,1,64]{2,0,1:T(4,128)S(1)}, f32[3,1,64]{2,0,1:T(4,128)S(1)}, u32[]{:S(2)}, u32[]{:S(2)}) %collective-permute-start.1) | collective-permute-done | bytes 800 | tf_op jit(solution)/shard_map/ppermute | solution.py:27
  26.5 1.9 collective-permute-done.3
  29.3 71.4 %while.26 = (s32[]{:T(128)}, f32[2,3,32,128]{3,1,2,0:T(4,128)}, f32[2,32,128]{2,0,1:T(2,128)S(1)}, s32[2,32,128]{2,1,0:T(8,128)}, f32[3,768]{0,1:T(8,128)S(1)}, ...) while((s32[]{:T(128)}, f32[2,3,32,128]{3,1,2,0:T(4,128)}, ...), condition=%wide.region_3.5_spmd, body=%wide.region_0.4_spmd.sunk | while | flops 271267840 | bytes 53851500 | solution.py:202
  30.2 10.8 %gather_fusion = f32[4096,3]{1,0:T(8,128)S(1)} fusion(f32[3,768]{0,1:T(8,128)S(1)} %get-tuple-element.926, s32[4096]{0:T(1024)S(1)} %bitcast_clamp_fusion.4), kind=kCustom, calls=%fused_computation.clone.clone.1 | custom fusion | bytes 114688 | tf_op jit(solution)/shard_map/while/body/eval_jaxpr/jit(_take)/gather | solution.py:194
  43.5 2.1 maximum_add_fusion.6
  55.3 1.8 copy.200
  65.9 10.8 %gather_fusion = f32[4096,3]{1,0:T(8,128)S(1)} fusion(f32[3,768]{0,1:T(8,128)S(1)} %get-tuple-element.926, s32[4096]{0:T(1024)S(1)} %bitcast_clamp_fusion.4), kind=kCustom, calls=%fused_computation.clone.clone.1 | custom fusion | bytes 114688 | tf_op jit(solution)/shard_map/while/body/eval_jaxpr/jit(_take)/gather | solution.py:194
  79.2 2.1 maximum_add_fusion.6
  91.0 1.8 copy.200
  100.7 3.5 copy.108
  104.2 45.3 %scatter_custom_fusion = f32[3,768]{0,1:T(8,128)S(1)} fusion(s32[8192]{0:T(1024)} %get-tuple-element.633, f32[8192,3]{1,0:T(8,128)} %bitcast.466, f32[]{:T(128)} %constant.182.clone.1), kind=kCustom, calls=%fused_computation.191 | custom fusion | flops 24576 | bytes 9728 | tf_op jit(solution)/shard_map/scatter-add | solution.py:213
  150.8 22.9 %reduce-scatter.7.cloned.1.call-done = f32[64,9]{1,0:T(8,128)} async-done(((f32[256,9]{1,0:T(8,128)}), f32[64,9]{1,0:T(8,128)}) %reduce-scatter.7.cloned.1.call-update) | async-done | bytes 2320
  176.0 2.7 collective-permute-done.5
  179.3 3.8 %collective-permute-start.9 = (f32[3,1,64]{2,0,1:T(4,128)S(1)}, f32[3,1,64]{2,0,1:T(4,128)S(1)}, u32[]{:S(2)}, u32[]{:S(2)}) collective-permute-start(f32[3,1,64]{2,0,1:T(4,128)S(1)} %bitcast.491), channel_id=1, source_target_pairs={{1,0},{2,1},{3,2},{0,3},{5,4},{6,5},{7,6},{4,7},{9,8},{10,9},{11,1... | collective-permute-start | bytes 2312 | tf_op jit(solution)/shard_map/ppermute | solution.py:29
  184.7 5.4 %collective-permute-done.8 = f32[3,1,64]{2,0,1:T(4,128)S(1)} collective-permute-done((f32[3,1,64]{2,0,1:T(4,128)S(1)}, f32[3,1,64]{2,0,1:T(4,128)S(1)}, u32[]{:S(2)}, u32[]{:S(2)}) %collective-permute-start.8) | collective-permute-done | bytes 800 | tf_op jit(solution)/shard_map/ppermute | solution.py:27
  192.1 2.6 collective-permute-done.10
  196.4 77.5 %while.27 = (s32[]{:T(128)}, f32[2,32]{1,0:T(2,128)}, f32[2,3,32,128]{3,1,2,0:T(4,128)}, f32[2,32,128]{2,0,1:T(2,128)S(1)}, s32[2,32,128]{2,1,0:T(8,128)}, /*ind...) while((s32[]{:T(128)}, f32[2,32]{1,0:T(2,128)}, ...), condition=%wide.region_10.12_spmd, body=%wide.region_7.11_spmd.sunk | while | flops 271367680 | bytes 45020100 | solution.py:202
  197.2 11.8 %gather_fusion.1 = f32[4096,3]{1,0:T(8,128)S(1)} fusion(f32[3,768]{0,1:T(8,128)} %get-tuple-element.988, s32[4096]{0:T(1024)S(1)} %bitcast_clamp_fusion.5), kind=kCustom, calls=%fused_computation.1.clone.clone.1 | custom fusion | bytes 114688 | tf_op jit(solution)/shard_map/while/body/eval_jaxpr/jit(_take)/gather | solution.py:194
  211.6 2.1 maximum_add_fusion.7
  222.9 2.4 fusion.309
  225.3 1.7 copy.208
  227.9 1.6 fusion.312
  235.9 11.8 %gather_fusion.1 = f32[4096,3]{1,0:T(8,128)S(1)} fusion(f32[3,768]{0,1:T(8,128)} %get-tuple-element.988, s32[4096]{0:T(1024)S(1)} %bitcast_clamp_fusion.5), kind=kCustom, calls=%fused_computation.1.clone.clone.1 | custom fusion | bytes 114688 | tf_op jit(solution)/shard_map/while/body/eval_jaxpr/jit(_take)/gather | solution.py:194
  250.3 2.1 maximum_add_fusion.7
  261.7 2.4 fusion.309
  264.0 1.7 copy.208
  273.9 3.5 copy.116
  277.4 45.2 %scatter_custom_fusion.1 = f32[3,768]{0,1:T(8,128)S(1)} fusion(s32[8192]{0:T(1024)} %get-tuple-element.633, f32[8192,3]{1,0:T(8,128)} %bitcast.465, f32[]{:T(128)} %constant.182.clone.1), kind=kCustom, calls=%fused_computation.189 | custom fusion | flops 24576 | bytes 9728 | tf_op jit(solution)/shard_map/scatter-add | solution.py:213
  323.8 22.9 %reduce-scatter.9.cloned.1.call-done = f32[64,9]{1,0:T(8,128)} async-done(((f32[256,9]{1,0:T(8,128)}), f32[64,9]{1,0:T(8,128)}) %reduce-scatter.9.cloned.1.call-update) | async-done | bytes 2320
  349.9 1.8 collective-permute-done.12
  (435 shorter events, 100.0 us)
Async XLA Ops:
  7.2 166.5 %reduce-scatter.7.cloned.1.call-start = ((), (), s32[]{:S(2)}) async-start(), calls=%async_computation.2 | async-start | bytes 163840
  7.9 21.4 %copy-start.58 = (f32[3,64]{1,0:T(4,128)}, f32[3,64]{1,0:T(4,128)S(1)}, u32[]{:S(2)}) copy-start(f32[3,64]{1,0:T(4,128)S(1)} %multiply_add_fusion.2) | copy-start | bytes 2308
  7.9 10.5 %collective-permute-start.2 = (f32[3,1,64]{2,0,1:T(4,128)S(1)}, f32[3,1,64]{2,0,1:T(4,128)S(1)}, u32[]{:S(2)}, u32[]{:S(2)}) collective-permute-start(f32[3,1,64]{2,0,1:T(4,128)S(1)} %bitcast.487), channel_id=1, source_target_pairs={{1,0},{2,1},{3,2},{0,3},{5,4},{6,5},{7,6},{4,7},{9,8},{10,9},{11,1... | collective-permute-start | bytes 2312 | tf_op jit(solution)/shard_map/ppermute | solution.py:29
  13.0 5.4 %collective-permute-start = (f32[3,1,64]{2,0,1:T(4,128)S(1)}, f32[3,1,64]{2,0,1:T(4,128)S(1)}, u32[]{:S(2)}, u32[]{:S(2)}) collective-permute-start(f32[3,1,64]{2,0,1:T(4,128)S(1)} %bitcast.488), channel_id=1, source_target_pairs={{0,1},{1,2},{2,3},{3,0},{4,5},{5,6},{6,7},{7,4},{8,9},{9,10},{10,1... | collective-permute-start | bytes 2312 | tf_op jit(solution)/shard_map/ppermute | solution.py:27
  18.4 5.4 %collective-permute-start.1 = (f32[3,1,64]{2,0,1:T(4,128)S(1)}, f32[3,1,64]{2,0,1:T(4,128)S(1)}, u32[]{:S(2)}, u32[]{:S(2)}) collective-permute-start(f32[3,1,64]{2,0,1:T(4,128)S(1)} %collective-permute-done), channel_id=1, source_target_pairs={{0,1},{1,2},{2,3},{3,0},{4,5},{5,6},{6,7},{7,4},{8,9},{9,10},{10,1... | collective-permute-start | bytes 2312 | tf_op jit(solution)/shard_map/ppermute | solution.py:27
  24.5 2.1 collective-permute-start.4
  24.5 4.0 %collective-permute-start.3 = (f32[3,1,256]{2,1,0:T(1,128)S(1)}, f32[3,1,256]{2,1,0:T(1,128)S(1)}, u32[]{:S(2)}, u32[]{:S(2)}) collective-permute-start(f32[3,1,256]{2,1,0:T(1,128)S(1)} %reshape.353), channel_id=1, source_target_pairs={{0,4},{4,8},{8,12},{12,16},{16,20},{20,24},{24,28},{28,0},{1,5},{5... | collective-permute-start | bytes 9224 | tf_op jit(solution)/shard_map/ppermute | solution.py:43
  65.0 16.3 %copy-start.14 = (f32[3,768]{0,1:T(8,128)}, f32[3,768]{0,1:T(8,128)S(1)}, u32[]{:S(2)}) copy-start(f32[3,768]{0,1:T(8,128)S(1)} %get-tuple-element.926) | copy-start | bytes 27652 | tf_op jit(solution)/shard_map/while
  104.2 71.1 %copy-start.49 = (f32[2,3,32,128]{3,1,2,0:T(4,128)S(1)}, f32[2,3,32,128]{3,1,2,0:T(4,128)}, u32[]{:S(2)}) copy-start(f32[2,3,32,128]{3,1,2,0:T(4,128)} %get-tuple-element.460) | copy-start | bytes 294916
  104.2 74.5 %copy-start.59 = (f32[3,64]{1,0:T(4,128)S(1)}, f32[3,64]{1,0:T(4,128)}, u32[]{:S(2)}) copy-start(f32[3,64]{1,0:T(4,128)} %copy-done.58) | copy-start | bytes 2308
  104.2 74.5 %copy-start.62 = (f32[3,64]{1,0:T(4,128)S(1)}, f32[3,64]{1,0:T(4,128)}, u32[]{:S(2)}) copy-start(f32[3,64]{1,0:T(4,128)} %param.22) | copy-start | bytes 2308
  104.2 74.5 %copy-start.63 = (f32[3,64]{1,0:T(4,128)S(1)}, f32[3,64]{1,0:T(4,128)}, u32[]{:S(2)}) copy-start(f32[3,64]{1,0:T(4,128)} %param.23) | copy-start | bytes 2308
  104.2 92.2 %copy-start.1 = (bf16[2048,240]{0,1:T(8,128)(2,1)S(1)}, bf16[2048,240]{0,1:T(8,128)(2,1)}, u32[]{:S(2)}) copy-start(bf16[2048,240]{0,1:T(8,128)(2,1)} %get-tuple-element.1006) | copy-start | bytes 2949124
  104.2 92.2 %copy-start.8 = (bf16[240,240]{1,0:T(8,128)(2,1)S(1)}, bf16[240,240]{1,0:T(8,128)(2,1)}, u32[]{:S(2)}) copy-start(bf16[240,240]{1,0:T(8,128)(2,1)} %get-tuple-element.1007) | copy-start | bytes 345604
  104.2 92.2 %copy-start.35 = (bf16[32,64]{1,0:T(8,128)(2,1)S(1)}, bf16[32,64]{1,0:T(8,128)(2,1)}, u32[]{:S(2)}) copy-start(bf16[32,64]{1,0:T(8,128)(2,1)} %get-tuple-element.1008) | copy-start | bytes 12292
  150.7 196.0 %reduce-scatter.9.cloned.1.call-start = ((), (), s32[]{:S(2)}) async-start(), calls=%async_computation.3 | async-start | bytes 163840
  174.7 1.3 collective-permute-start.6
  174.8 3.9 %collective-permute-start.5 = (f32[3,1,64]{2,0,1:T(4,128)S(1)}, f32[3,1,64]{2,0,1:T(4,128)S(1)}, u32[]{:S(2)}, u32[]{:S(2)}) collective-permute-start(f32[3,1,64]{2,0,1:T(4,128)S(1)} %copy.135), channel_id=1, source_target_pairs={{0,4},{4,8},{8,12},{12,16},{16,20},{20,24},{24,28},{28,0},{1,5},{5... | collective-permute-start | bytes 2312 | tf_op jit(solution)/shard_map/ppermute | solution.py:43
  179.3 17.2 %copy-start.60 = (f32[3,64]{1,0:T(4,128)}, f32[3,64]{1,0:T(4,128)S(1)}, u32[]{:S(2)}) copy-start(f32[3,64]{1,0:T(4,128)S(1)} %get-tuple-element.613) | copy-start | bytes 2308
  179.3 5.4 %collective-permute-start.7 = (f32[3,1,64]{2,0,1:T(4,128)S(1)}, f32[3,1,64]{2,0,1:T(4,128)S(1)}, u32[]{:S(2)}, u32[]{:S(2)}) collective-permute-start(f32[3,1,64]{2,0,1:T(4,128)S(1)} %bitcast.490), channel_id=1, source_target_pairs={{0,1},{1,2},{2,3},{3,0},{4,5},{5,6},{6,7},{7,4},{8,9},{9,10},{10,1... | collective-permute-start | bytes 2312 | tf_op jit(solution)/shard_map/ppermute | solution.py:27
  179.3 5.4 %collective-permute-start.9 = (f32[3,1,64]{2,0,1:T(4,128)S(1)}, f32[3,1,64]{2,0,1:T(4,128)S(1)}, u32[]{:S(2)}, u32[]{:S(2)}) collective-permute-start(f32[3,1,64]{2,0,1:T(4,128)S(1)} %bitcast.491), channel_id=1, source_target_pairs={{1,0},{2,1},{3,2},{0,3},{5,4},{6,5},{7,6},{4,7},{9,8},{10,9},{11,1... | collective-permute-start | bytes 2312 | tf_op jit(solution)/shard_map/ppermute | solution.py:29
  184.7 5.4 %collective-permute-start.8 = (f32[3,1,64]{2,0,1:T(4,128)S(1)}, f32[3,1,64]{2,0,1:T(4,128)S(1)}, u32[]{:S(2)}, u32[]{:S(2)}) collective-permute-start(f32[3,1,64]{2,0,1:T(4,128)S(1)} %collective-permute-done.7), channel_id=1, source_target_pairs={{0,1},{1,2},{2,3},{3,0},{4,5},{5,6},{6,7},{7,4},{8,9},{9,10},{10,1... | collective-permute-start | bytes 2312 | tf_op jit(solution)/shard_map/ppermute | solution.py:27
  190.8 1.3 collective-permute-start.11
  190.8 4.0 %collective-permute-start.10 = (f32[3,1,256]{2,1,0:T(1,128)S(1)}, f32[3,1,256]{2,1,0:T(1,128)S(1)}, u32[]{:S(2)}, u32[]{:S(2)}) collective-permute-start(f32[3,1,256]{2,1,0:T(1,128)S(1)} %reshape.359), channel_id=1, source_target_pairs={{0,4},{4,8},{8,12},{12,16},{16,20},{20,24},{24,28},{28,0},{1,5},{5... | collective-permute-start | bytes 9224 | tf_op jit(solution)/shard_map/ppermute | solution.py:43
  196.5 17.2 %copy-start.38 = (f32[2,32,128]{2,0,1:T(2,128)}, f32[2,32,128]{2,0,1:T(2,128)S(1)}, u32[]{:S(2)}) copy-start(f32[2,32,128]{2,0,1:T(2,128)S(1)} %get-tuple-element.986) | copy-start | bytes 98308 | tf_op jit(solution)/shard_map/while
  196.5 17.2 %copy-start.42 = (f32[2,32,128]{2,0,1:T(2,128)}, f32[2,32,128]{2,0,1:T(2,128)S(1)}, u32[]{:S(2)}) copy-start(f32[2,32,128]{2,0,1:T(2,128)S(1)} %get-tuple-element.990) | copy-start | bytes 98308 | tf_op jit(solution)/shard_map/while
  235.2 17.2 %copy-start.38 = (f32[2,32,128]{2,0,1:T(2,128)}, f32[2,32,128]{2,0,1:T(2,128)S(1)}, u32[]{:S(2)}) copy-start(f32[2,32,128]{2,0,1:T(2,128)S(1)} %get-tuple-element.986) | copy-start | bytes 98308 | tf_op jit(solution)/shard_map/while
  235.2 17.2 %copy-start.42 = (f32[2,32,128]{2,0,1:T(2,128)}, f32[2,32,128]{2,0,1:T(2,128)S(1)}, u32[]{:S(2)}) copy-start(f32[2,32,128]{2,0,1:T(2,128)S(1)} %get-tuple-element.990) | copy-start | bytes 98308 | tf_op jit(solution)/shard_map/while
  277.4 70.9 %copy-start.46 = (f32[2,3,32,128]{3,1,2,0:T(4,128)S(1)}, f32[2,3,32,128]{3,1,2,0:T(4,128)}, u32[]{:S(2)}) copy-start(f32[2,3,32,128]{3,1,2,0:T(4,128)} %get-tuple-element.461) | copy-start | bytes 294916
  277.4 74.3 %copy-start.61 = (f32[3,64]{1,0:T(4,128)S(1)}, f32[3,64]{1,0:T(4,128)}, u32[]{:S(2)}) copy-start(f32[3,64]{1,0:T(4,128)} %get-tuple-element.614) | copy-start | bytes 2308
  347.7 2.2 collective-permute-start.13
  347.8 3.9 %collective-permute-start.12 = (f32[3,1,64]{2,0,1:T(4,128)S(1)}, f32[3,1,64]{2,0,1:T(4,128)S(1)}, u32[]{:S(2)}, u32[]{:S(2)}) collective-permute-start(f32[3,1,64]{2,0,1:T(4,128)S(1)} %copy.138), channel_id=1, source_target_pairs={{0,4},{4,8},{8,12},{12,16},{16,20},{20,24},{24,28},{28,0},{1,5},{5... | collective-permute-start | bytes 2312 | tf_op jit(solution)/shard_map/ppermute | solution.py:43
  (102 other events, 414.8 us)
Sparse Core Ops, SparseCore 0:
  150.8 22.7 reduce-scatter.6
  323.9 22.7 reduce-scatter.8
